TPU v7x, 32 devices: a whole 2x2x4 slice. The times are simulated.
32 devices in a mesh: prow: 4 (over x, core), pcol: 8 (over z, y).
Axes of the slice: x: 2, y: 2, z: 4, core: 2. Of those that a mesh axis runs over, the one named last changes fastest.
Arguments:
- coords: int32 [3, 8192], P(None, ('prow', 'pcol')), may hold values from 0 to 1023
- block_map: int32 [64], replicated, may hold values from 0 to 63, each once
- pattern: int32 [2, 64], replicated, may hold values 0 or 1
Outputs:
- factor: float32 [16, 4, 128, 8, 8, 128], P(None, 'prow', None, None, 'pcol')
Inputs may be any that keep to these rules, and one draw needn't show every extreme that they name: `block_map`: every block number appears once.
All inputs are finite; a program needn't handle non-finite values.
Results may differ from a plain program's by a relative error of at most 0.0001.
Values sent between devices are 32-bit elements; how exact they have to be, the bound alone decides.
No kernel may reach another device: no remote copies, remote signals or barrier semaphores. Data moves between devices by JAX's collectives and lax.ppermute only.
A program may use at most 128 MiB of HBM per device.

v0:
```python
import jax
import jax.numpy as jnp
from jax import lax
from jax.sharding import PartitionSpec as P

BLOCK = 128
SNODE_BLOCKS = 4
PANELS = 2


spread_factor = 89.0
scale_gain = 8.0


def spread_2(value, axis, source):
    kept = jnp.where(lax.axis_index(axis) == source, value, 0).astype(value.dtype)
    return lax.psum(kept, axis)


def lookup(table, index):
    spots = jnp.arange(table.shape[-1], dtype=jnp.int32)
    return jnp.sum(jnp.where(index[..., None] == spots, table, 0), axis=-1)


def member(panel_at, ids, pattern):
    first = panel_at * SNODE_BLOCKS
    stop = first + SNODE_BLOCKS
    value = lookup(pattern[panel_at], ids)
    own = (ids >= first) & (ids < stop)
    before = ids < first
    return jnp.where(own, 1, jnp.where(before, 0, value)).astype(jnp.float32)


def block_mask(row_ids, col_ids, pattern):
    weight = (row_ids[:, None] == col_ids[None, :]).astype(jnp.float32)
    for panel_at in range(PANELS):
        row_in = member(panel_at, row_ids, pattern)
        col_in = member(panel_at, col_ids, pattern)
        weight = weight + row_in[:, None] * col_in[None, :]
    return weight


def wendland(dist_sq, radius):
    ratio = jnp.sqrt(dist_sq) / radius
    rest = jnp.maximum(1.0 - ratio, 0.0)
    rest_sq = rest * rest
    return rest_sq * rest_sq * rest_sq * ((35.0 * ratio + 18.0) * ratio + 3.0) * (1.0 / 3.0)


def local(coords, block_map, pattern):
    rows_n = lax.axis_size("prow")
    cols_n = lax.axis_size("pcol")
    prow_at = lax.axis_index("prow")
    pcol_at = lax.axis_index("pcol")
    nblocks = block_map.shape[0]
    row_count = nblocks // rows_n
    col_count = nblocks // cols_n
    front = nblocks * BLOCK
    width = SNODE_BLOCKS * BLOCK
    radius = (spread_factor / front) ** (1.0 / 3.0)
    all_points = lax.all_gather(coords, ("prow", "pcol"), axis=1, tiled=True)
    inverse = (
        jnp.zeros((nblocks,), jnp.int32).at[block_map].set(jnp.arange(nblocks, dtype=jnp.int32))
    )
    placed = all_points.reshape(3, nblocks, BLOCK)[:, inverse, :]
    points = placed.astype(jnp.float32) * (1.0 / 1024.0)
    row_pts = lax.dynamic_index_in_dim(
        points.reshape(3, row_count, rows_n, BLOCK), prow_at, 2, keepdims=False
    )
    col_pts = lax.dynamic_index_in_dim(
        points.reshape(3, col_count, cols_n, BLOCK), pcol_at, 2, keepdims=False
    )
    row_ids = jnp.arange(row_count, dtype=jnp.int32) * rows_n + prow_at
    col_ids = jnp.arange(col_count, dtype=jnp.int32) * cols_n + pcol_at
    dist = (row_pts[0][:, :, None, None] - col_pts[0][None, None, :, :]) ** 2
    dist = dist + (row_pts[1][:, :, None, None] - col_pts[1][None, None, :, :]) ** 2
    dist = dist + (row_pts[2][:, :, None, None] - col_pts[2][None, None, :, :]) ** 2
    mask = block_mask(row_ids, col_ids, pattern)
    coupling = wendland(dist, radius) * mask[:, None, :, None]
    row_part = jnp.sum(coupling, axis=(2, 3))
    col_part = jnp.sum(coupling, axis=(0, 1))
    row_total = lax.psum(row_part, "pcol")
    col_total = lax.psum(col_part, "prow")
    row_scale = scale_gain * lax.rsqrt(1.0 + row_total)
    col_scale = scale_gain * lax.rsqrt(1.0 + col_total)
    same_block = (row_ids[:, None] == col_ids[None, :])[:, None, :, None]
    same_cell = (jnp.arange(BLOCK)[:, None] == jnp.arange(BLOCK)[None, :])[None, :, None, :]
    matrix = coupling * row_scale[:, :, None, None] * col_scale[None, None, :, :]
    matrix = matrix + (same_block & same_cell).astype(jnp.float32)
    for panel_at in range(PANELS):
        first = panel_at * SNODE_BLOCKS
        stop = first + SNODE_BLOCKS
        owner_block = first // cols_n
        column_piece = matrix[:, :, owner_block, :]
        spread = lax.all_gather(column_piece, "pcol", axis=2, tiled=True)
        begin = first % cols_n * BLOCK
        panel = spread[:, :, begin : begin + width]
        offset = (prow_at - first) % rows_n
        valid = (offset < SNODE_BLOCKS).astype(jnp.float32)
        local_row = jnp.minimum((first + offset) // rows_n, row_count - 1)
        piece = lax.dynamic_index_in_dim(panel, local_row, 0, keepdims=False) * valid
        stacked = lax.all_gather(piece, "prow", axis=0, tiled=True)
        diagonal = jnp.concatenate(
            [
                stacked[(first + step) % rows_n * BLOCK : ((first + step) % rows_n + 1) * BLOCK]
                for step in range(SNODE_BLOCKS)
            ],
            axis=0,
        )
        lower = jnp.linalg.cholesky(diagonal)
        flat = panel.reshape(row_count * BLOCK, width)
        solved = lax.linalg.triangular_solve(
            lower, flat, left_side=False, lower=True, transpose_a=True
        )
        factor_rows = (
            solved.reshape(row_count, BLOCK, width)
            * (row_ids >= first).astype(jnp.float32)[:, None, None]
        )
        trail_rows = factor_rows * (row_ids >= stop).astype(jnp.float32)[:, None, None]
        chosen = factor_rows[col_ids // rows_n]
        root = pcol_at % rows_n
        col_rows = spread_2(chosen, "prow", root)
        col_trail = col_rows * (col_ids >= stop).astype(jnp.float32)[:, None, None]
        update = jnp.einsum("aik,cjk->aicj", trail_rows, col_trail, precision=lax.Precision.HIGHEST)
        matrix = matrix - update
        in_panel = (col_ids >= first) & (col_ids < stop)
        which = jnp.clip(col_ids - first, 0, SNODE_BLOCKS - 1)
        taken = jnp.take(factor_rows.reshape(row_count, BLOCK, SNODE_BLOCKS, BLOCK), which, axis=2)
        matrix = jnp.where(in_panel[None, None, :, None], taken, matrix)
        row_in = (row_ids >= first) & (row_ids < stop)
        upper = row_in[:, None] & (col_ids >= stop)[None, :]
        matrix = jnp.where(upper[:, None, :, None], 0.0, matrix)
    return matrix.reshape(row_count, 1, BLOCK, col_count, 1, BLOCK)


def solution(mesh):
    placed = (P(None, ("prow", "pcol")), P(), P())
    return jax.shard_map(
        local,
        mesh=mesh,
        in_specs=placed,
        out_specs=P(None, "prow", None, None, "pcol", None),
        check_vma=False,
    )
```

profile of v0, /device:TPU:0, one launch (start us, length us, event | category | flops | bytes accessed | tf_op | source)
XLA Modules:
  0.0 940.7 jit_solution(6668163431641681821)
XLA Ops:
  8.0 70.7 %all_gather.15 = s32[3,8192]{1,0:T(4,128)S(1)} all-gather(s32[3,256]{1,0:T(4,128)} %param.8), channel_id=1, replica_groups=mesh['prow'=4,'pcol'=8] {'prow','pcol'}, dimensions={1}, use_global_device_ids=true | all-gather | bytes 101376 | tf_op jit(solution)/shard_map/all_gather | solution.py:61
  80.8 8.7 fusion.12
  89.5 17.4 %psum.28 = f32[16,128]{1,0:T(8,128)S(1)} all-reduce(f32[16,128]{1,0:T(8,128)S(1)} %get-tuple-element.24), channel_id=1, replica_groups=mesh['prow'=4,'pcol'=8] {'pcol'}, use_global_device_ids=true, to_apply=%region_6.7 | all-reduce | flops 2048 | bytes 16384 | tf_op jit(solution)/shard_map/psum | solution.py:82
  112.9 9.8 %convert_add_fusion = f32[16,128,8,128]{1,3,0,2:T(8,128)S(1)} fusion(f32[8,128]{1,0:T(8,128)S(1)} %rsqrt_multiply_fusion.1, f32[16,128]{1,0:T(8,128)S(1)} %rsqrt_multiply_fusion, f32[16,8]{0,1:T(8,128)S(1)} %add_multiply_fusion, f32[8,128]{1,0:T(8,128)S(1)} %bitcast.216, f32[16,128]{1,0:T(8,128)S(1)} %bitcast.207, f32[8,128]{1,0:T(8,128)S(1)} %bitcast.213, ...), kind=kLoop, calls=%fused_computation.18 | loop fusion | flops 52428800 | bytes 8454784 | tf_op jit(solution)/shard_map/add | solution.py:89
  123.9 122.2 %all-gather.9.cloned.1.call-done = f32[16,128,1,1024]{1,3,0,2:T(8,128)} async-done(((f32[16,128,1,128]{1,3,0,2:T(8,128)}), f32[16,128,1,1024]{1,3,0,2:T(8,128)}) %all-gather.9.cloned.1.call-update) | async-done | bytes 8388624 | tf_op jit(solution)/shard_map/all_gather | solution.py:95
  257.1 9.5 %all-gather.11.cloned.1.call-done = f32[1,512,512]{1,2,0:T(8,128)} async-done(((f32[1,128,512]{1,2,0:T(8,128)}), f32[1,512,512]{1,2,0:T(8,128)}) %all-gather.11.cloned.1.call-update) | async-done | bytes 1048592 | tf_op jit(solution)/shard_map/all_gather | solution.py:102
  269.6 11.7 %cholesky.286 = f32[128,128]{1,0:T(8,128)S(1)} custom-call(f32[128,128]{1,0:T(8,128)S(1)} %cholesky.426), custom_call_target="Cholesky" | custom-call | tf_op jit(solution)/shard_map/jit(cholesky)/cholesky | solution.py:110
  281.5 9.8 %custom-call.27 = f32[1,128,128]{1,2,0:T(8,128)S(1)} custom-call(f32[1,128,128]{2,1,0:T(8,128)S(1)} %get-tuple-element.79), custom_call_target="InvertDiagBlocksLowerTriangular" | custom-call | tf_op jit(solution)/shard_map/jit(cholesky)/cholesky | solution.py:110
  292.0 11.7 %cholesky.305 = f32[128,128]{1,0:T(8,128)S(1)} custom-call(f32[128,128]{1,0:T(8,128)S(1)} %cholesky.430), custom_call_target="Cholesky" | custom-call | tf_op jit(solution)/shard_map/jit(cholesky)/cholesky | solution.py:110
  305.0 10.2 %custom-call.28 = f32[1,128,128]{1,2,0:T(8,128)S(1)} custom-call(f32[1,128,128]{2,1,0:T(8,128)S(1)} %get-tuple-element.76), custom_call_target="InvertDiagBlocksLowerTriangular" | custom-call | tf_op jit(solution)/shard_map/jit(cholesky)/cholesky | solution.py:110
  315.9 11.7 %cholesky.326 = f32[128,128]{1,0:T(8,128)S(1)} custom-call(f32[128,128]{1,0:T(8,128)S(1)} %cholesky.435), custom_call_target="Cholesky" | custom-call | tf_op jit(solution)/shard_map/jit(cholesky)/cholesky | solution.py:110
  328.3 9.8 %custom-call.29 = f32[1,128,128]{1,2,0:T(8,128)S(1)} custom-call(f32[1,128,128]{2,1,0:T(8,128)S(1)} %get-tuple-element.73), custom_call_target="InvertDiagBlocksLowerTriangular" | custom-call | tf_op jit(solution)/shard_map/jit(cholesky)/cholesky | solution.py:110
  338.7 11.7 %cholesky.343 = f32[128,128]{1,0:T(8,128)S(1)} custom-call(f32[128,128]{1,0:T(8,128)S(1)} %convolution_subtract_fusion.9), custom_call_target="Cholesky" | custom-call | tf_op jit(solution)/shard_map/jit(cholesky)/cholesky | solution.py:110
  362.0 39.3 %custom-call.30 = f32[4,128,128]{1,2,0:T(8,128)S(1)} custom-call(f32[4,128,128]{2,1,0:T(8,128)S(1)} %get-tuple-element.22), custom_call_target="InvertDiagBlocksLowerTriangular" | custom-call | tf_op jit(solution)/shard_map/triangular_solve/custom-call.3 | solution.py:112
  462.9 9.2 copy.31
  472.0 20.2 %all-reduce.4.cloned.1.call-done = f32[8,128,512]{2,1,0:T(8,128)} async-done(((f32[8,128,512]{2,1,0:T(8,128)}), f32[8,128,512]{2,1,0:T(8,128)}) %all-reduce.4.cloned.1.call-update) | async-done | bytes 2097168 | tf_op jit(solution)/shard_map/psum | solution.py:17
  492.2 26.2 %fusion.4 = f32[16,128,8,128]{1,3,0,2:T(8,128)S(1)} fusion(f32[8,16,128,128]{2,3,1,0:T(8,128)} %copy.31, pred[8]{0:T(512)(128)(4,1)S(1)} %get-tuple-element.88, pred[8]{0:T(512)(128)(4,1)S(1)} %get-tuple-element.89, pred[16,8]{0,1:T(8,128)(4,1)S(1)} %broadcast_and_fusion, f32[8,128,512]{2,1,0:T(8,128)} %all-reduce.4.cloned.1.call-done, ...), kind=kOutput, calls=%fused_computation.17 | convolution fusion | flops 12947292160 | bytes 23135088 | tf_op jit(solution)/shard_map/aik,cjk->aicj/dot_general | solution.py:124
  522.9 124.6 %all-gather.13.cloned.1.call-done = f32[16,128,1,1024]{1,3,0,2:T(8,128)} async-done(((f32[16,128,1,128]{1,3,0,2:T(8,128)}), f32[16,128,1,1024]{1,3,0,2:T(8,128)}) %all-gather.13.cloned.1.call-update) | async-done | bytes 8388624 | tf_op jit(solution)/shard_map/all_gather | solution.py:95
  658.3 9.6 %all-gather.15.cloned.1.call-done = f32[1,512,512]{1,2,0:T(8,128)} async-done(((f32[1,128,512]{1,2,0:T(8,128)}), f32[1,512,512]{1,2,0:T(8,128)}) %all-gather.15.cloned.1.call-update) | async-done | bytes 1048592 | tf_op jit(solution)/shard_map/all_gather | solution.py:102
  670.9 11.7 %cholesky.358 = f32[128,128]{1,0:T(8,128)S(1)} custom-call(f32[128,128]{1,0:T(8,128)S(1)} %cholesky.439), custom_call_target="Cholesky" | custom-call | tf_op jit(solution)/shard_map/jit(cholesky)/cholesky | solution.py:110
  682.8 9.8 %custom-call.31 = f32[1,128,128]{1,2,0:T(8,128)S(1)} custom-call(f32[1,128,128]{2,1,0:T(8,128)S(1)} %get-tuple-element.69), custom_call_target="InvertDiagBlocksLowerTriangular" | custom-call | tf_op jit(solution)/shard_map/jit(cholesky)/cholesky | solution.py:110
  693.3 11.7 %cholesky.377 = f32[128,128]{1,0:T(8,128)S(1)} custom-call(f32[128,128]{1,0:T(8,128)S(1)} %cholesky.443), custom_call_target="Cholesky" | custom-call | tf_op jit(solution)/shard_map/jit(cholesky)/cholesky | solution.py:110
  706.3 10.2 %custom-call.32 = f32[1,128,128]{1,2,0:T(8,128)S(1)} custom-call(f32[1,128,128]{2,1,0:T(8,128)S(1)} %get-tuple-element.66), custom_call_target="InvertDiagBlocksLowerTriangular" | custom-call | tf_op jit(solution)/shard_map/jit(cholesky)/cholesky | solution.py:110
  717.2 11.7 %cholesky.398 = f32[128,128]{1,0:T(8,128)S(1)} custom-call(f32[128,128]{1,0:T(8,128)S(1)} %cholesky.448), custom_call_target="Cholesky" | custom-call | tf_op jit(solution)/shard_map/jit(cholesky)/cholesky | solution.py:110
  729.7 9.8 %custom-call.33 = f32[1,128,128]{1,2,0:T(8,128)S(1)} custom-call(f32[1,128,128]{2,1,0:T(8,128)S(1)} %get-tuple-element.63), custom_call_target="InvertDiagBlocksLowerTriangular" | custom-call | tf_op jit(solution)/shard_map/jit(cholesky)/cholesky | solution.py:110
  740.1 11.7 %cholesky.415 = f32[128,128]{1,0:T(8,128)S(1)} custom-call(f32[128,128]{1,0:T(8,128)S(1)} %convolution_subtract_fusion.8), custom_call_target="Cholesky" | custom-call | tf_op jit(solution)/shard_map/jit(cholesky)/cholesky | solution.py:110
  755.4 7.9 while.5
  763.3 39.3 %custom-call.34 = f32[4,128,128]{1,2,0:T(8,128)S(1)} custom-call(f32[4,128,128]{2,1,0:T(8,128)S(1)} %get-tuple-element.23), custom_call_target="InvertDiagBlocksLowerTriangular" | custom-call | tf_op jit(solution)/shard_map/triangular_solve/custom-call.3 | solution.py:112
  864.3 9.2 copy.37
  873.5 20.2 %all-reduce.6.cloned.1.call-done = f32[8,128,512]{2,1,0:T(8,128)} async-done(((f32[8,128,512]{2,1,0:T(8,128)}), f32[8,128,512]{2,1,0:T(8,128)}) %all-reduce.6.cloned.1.call-update) | async-done | bytes 2097168 | tf_op jit(solution)/shard_map/psum | solution.py:17
  893.6 19.5 %fusion.3 = f32[16,1,128,8,1,128]{2,5,0,3,4,1:T(8,128)} fusion(f32[8,16,128,128]{2,3,1,0:T(8,128)} %copy.37, f32[16,128,8,128]{1,3,0,2:T(8,128)} %copy-done.2, pred[8]{0:T(512)(128)(4,1)S(1)} %get-tuple-element.94, pred[8]{0:T(512)(128)(4,1)S(1)} %get-tuple-element.95, pred[16,8]{0,1:T(8,128)(4,1)S(1)} %broadcast_and_fusion.1, ...), kind=kOutput, calls=%fused_computation.15 | convolution fusion | flops 12894863360 | bytes 31457520 | tf_op jit(solution)/shard_map/aik,cjk->aicj/dot_general | solution.py:124
  913.1 20.5 %copy.40 = f32[16,1,128,8,1,128]{5,4,3,2,1,0:T(1,128)} copy(f32[16,1,128,8,1,128]{2,5,0,3,4,1:T(8,128)} %fusion.3) | data formatting | bytes 16777216 | tf_op jit(solution)/shard_map/reshape | solution.py:133
  (167 shorter events, 199.5 us)
Async XLA Ops:
  6.5 239.6 %all-gather.9.cloned.1.call-start = ((), (), s32[]{:S(2)}) async-start(), calls=%async_computation.2 | async-start | bytes 9437184 | tf_op jit(solution)/shard_map/all_gather | solution.py:95
  123.8 142.7 %all-gather.11.cloned.1.call-start = ((), (), s32[]{:S(2)}) async-start(), calls=%async_computation.3 | async-start | bytes 1310720 | tf_op jit(solution)/shard_map/all_gather | solution.py:102
  248.7 2.0 copy-start
  251.4 240.8 %all-reduce.4.cloned.1.call-start = ((), (), s32[]{:S(2)}) async-start(), calls=%async_computation | async-start | bytes 4194304 | tf_op jit(solution)/shard_map/psum | solution.py:17
  440.7 206.8 %all-gather.13.cloned.1.call-start = ((), (), s32[]{:S(2)}) async-start(), calls=%async_computation.4 | async-start | bytes 9437184 | tf_op jit(solution)/shard_map/all_gather | solution.py:95
  518.5 3.2 copy-start.2
  522.8 145.1 %all-gather.15.cloned.1.call-start = ((), (), s32[]{:S(2)}) async-start(), calls=%async_computation.5 | async-start | bytes 1310720 | tf_op jit(solution)/shard_map/all_gather | solution.py:102
  650.0 2.0 copy-start.1
  652.7 240.9 %all-reduce.6.cloned.1.call-start = ((), (), s32[]{:S(2)}) async-start(), calls=%async_computation.1 | async-start | bytes 4194304 | tf_op jit(solution)/shard_map/psum | solution.py:17
Sparse Core Ops, SparseCore 0:
  124.0 122.1 all-gather.8
  251.5 14.9 all-gather.10
  440.8 51.3 all-reduce.3
  522.9 124.5 all-gather.12
  652.9 14.9 all-gather.14
  842.2 51.3 all-reduce.5
where the time goes:
time: 950 us; the launch traced here: 941 us
  waiting for transfers between devices  306 us (32%)
  other arithmetic  294 us (31%)
  local copies, waits for them, and re-layouts  136 us (14%)
  blocking collectives  94.1 us (10%)
  matrix products  89.9 us (9%)
  between operations  19.6 us (2%)
    all_gather x2, waiting for transfers between devices, local(): spread = lax.all_gather(column_piece, 'pcol', axis=2, tiled=True)  247 us
    another operation x30, other arithmetic, local(): lower = jnp.linalg.cholesky(diagonal)  159 us
    another operation x7, other arithmetic, local(): lax.linalg.triangular_solve(lower, flat, left_side=False, lower=True, tra...  88 us
    all_gather x1, blocking collectives, local(): all_points = lax.all_gather(coords, ('prow', 'pcol'), axis=1, tiled=True)  70.7 us
    dot_general x2, matrix products, local(): jnp.einsum('aik,cjk->aicj', trail_rows, col_trail, precision=lax.Precisio...  45.7 us
    another operation x14, matrix products, local(): lax.linalg.triangular_solve(lower, flat, left_side=False, lower=True, tra...  40.5 us
    psum x2, waiting for transfers between devices, spread_2(): return lax.psum(kept, axis)  40.3 us
    gather x4, local copies, waits for them, and re-layouts, local(): jnp.take(factor_rows.reshape(row_count, BLOCK, SNODE_BLOCKS, BLOCK), whic...  31.8 us
  transfers between devices with their start and end apart: 6, of which 6 were waited for; matrix products, arithmetic and copies ran while one was open for 8% of the time, Pallas kernels for 0%

commit v1 on v0

v1 whole, which is shorter than its diff:
```python
import functools

import jax
import jax.numpy as jnp
from jax import lax
from jax.experimental import pallas as pl
from jax.experimental.pallas import tpu as pltpu
from jax.sharding import PartitionSpec as P

BLOCK = 128
SNODE_BLOCKS = 4
PANELS = 2
LEAD = PANELS * SNODE_BLOCKS
WIDTH = SNODE_BLOCKS * BLOCK

spread_factor = 89.0
scale_gain = 8.0
grid_step = 1024.0

LOW, HIGH = 0.98, 66.0

f32 = jnp.float32
bf16 = jnp.bfloat16
NN = (((1,), (0,)), ((), ()))
NT = (((1,), (1,)), ((), ()))
TN = (((0,), (0,)), ((), ()))
FEATURES = 32
VMEM_BYTES = 60 * 1024 * 1024


def mm(a, b, dims):
    return lax.dot_general(a, b, dims, preferred_element_type=f32)


def split(a):
    high = a.astype(bf16)
    low = (a - high.astype(f32)).astype(bf16)
    return high, low


def dot1(a, b, dims=NN):
    return mm(a.astype(bf16), b.astype(bf16), dims)


def dot3(a, b, dims=NN):
    a_high, a_low = split(a)
    b_high, b_low = split(b)
    return mm(a_high, b_high, dims) + (mm(a_high, b_low, dims) + mm(a_low, b_high, dims))


def eye(n):
    return (lax.broadcasted_iota(jnp.int32, (n, n), 0) == lax.broadcasted_iota(jnp.int32, (n, n), 1)).astype(f32)


def newton(blocks, n):
    first = 2 / (LOW + HIGH)
    rho = (HIGH - LOW) / (HIGH + LOW)
    one = eye(n)
    step = 2 / (2 - rho * rho)
    rho = rho * rho / (2 - rho * rho)
    found = [(2 * step * first) * one - (step * first * first) * a for a in blocks]
    for at in range(5):
        dot = dot1 if at < 2 else dot3
        step = 2 / (2 - rho * rho) if at < 4 else 1.0
        rho = rho * rho / (2 - rho * rho)
        rest = [(2 * one) - dot(a, x) for a, x in zip(blocks, found)]
        found = [step * dot(x, e) for x, e in zip(found, rest)]
    return found


def chains(work, count):
    sub = lax.broadcasted_iota(jnp.int32, (8, BLOCK), 0)
    zero = jnp.zeros((8, BLOCK), f32)
    for strip in range(BLOCK // 8):
        at = 8 * strip
        state = []
        for b in range(count):
            r = work[b][at : at + 8, 0:BLOCK]
            y = work[b][at : at + 8, BLOCK : 2 * BLOCK]
            c = [jnp.broadcast_to(r[:, at + k : at + k + 1], (8, BLOCK)) for k in range(8)]
            state.append([r, y, c])
        for k in range(8):
            for b in range(count):
                r, y, c = state[b]
                inv = lax.rsqrt(c[k][k : k + 1, :])
                column = c[k] * inv
                below = jnp.where(sub > k, column, 0.0)
                r_row = r[k : k + 1] * inv
                y_row = y[k : k + 1] * inv
                r = jnp.where(sub == k, r_row, r - below * r_row)
                y = jnp.where(sub == k, y_row, y - below * y_row)
                for m in range(k + 1, 8):
                    c[m] = c[m] - below * column[m : m + 1, :]
                state[b] = [r, y, c]
        for b in range(count):
            r, y, _ = state[b]
            work[b][at : at + 8, 0:BLOCK] = r
            work[b][at : at + 8, BLOCK : 2 * BLOCK] = y
            if strip < BLOCK // 8 - 1:
                r_high = r.astype(bf16).astype(f32)
                y_high = y.astype(bf16).astype(f32)
                high = jnp.concatenate([r_high, y_high], 1)
                low = jnp.concatenate([r - r_high, y - y_high], 1)
                left = jnp.concatenate([r_high, r_high, r - r_high, zero], 0).astype(bf16)
                right = jnp.concatenate([high, low, high, jnp.concatenate([zero, zero], 1)], 0).astype(bf16)
                update = mm(left, right, TN)
                work[b][at + 8 :, :] = work[b][at + 8 :, :] - update[at + 8 :, :]


def factor_diagonal(a_ref, x_ref, work):
    half = 2 * BLOCK
    rows = lax.broadcasted_iota(jnp.int32, (BLOCK, BLOCK), 0)
    cols = lax.broadcasted_iota(jnp.int32, (BLOCK, BLOCK), 1)
    lower = cols <= rows
    a11 = a_ref[0:half, 0:half]
    a21 = a_ref[half:, 0:half]
    s2 = a_ref[half:, half:] - dot3(dot3(a21, newton([a11], half)[0]), a21, NT)
    corner = [a11[0:BLOCK, 0:BLOCK], s2[0:BLOCK, 0:BLOCK]]
    side = [a11[BLOCK:, 0:BLOCK], s2[BLOCK:, 0:BLOCK]]
    last = [a11[BLOCK:, BLOCK:], s2[BLOCK:, BLOCK:]]
    inverse = newton(corner, BLOCK)
    for i in range(2):
        work[2 * i][:, 0:BLOCK] = corner[i]
        work[2 * i + 1][:, 0:BLOCK] = last[i] - dot3(dot3(side[i], inverse[i]), side[i], NT)
    for b in range(4):
        work[b][:, BLOCK:] = eye(BLOCK)
    chains(work, 4)
    for i in range(2):
        at = half * i
        xa = jnp.where(lower, work[2 * i][:, BLOCK:], 0.0)
        xb = jnp.where(lower, work[2 * i + 1][:, BLOCK:], 0.0)
        l21 = dot3(side[i], xa, NT)
        x_ref[at : at + BLOCK, at : at + BLOCK] = xa
        x_ref[at : at + BLOCK, at + BLOCK : at + half] = jnp.zeros((BLOCK, BLOCK), f32)
        x_ref[at + BLOCK : at + half, at : at + BLOCK] = -dot3(xb, dot3(l21, xa))
        x_ref[at + BLOCK : at + half, at + BLOCK : at + half] = xb
    x11 = x_ref[0:half, 0:half]
    x22 = x_ref[half:, half:]
    l21 = dot3(a21, x11, NT)
    x_ref[half:, 0:half] = -dot3(x22, dot3(l21, x11))
    x_ref[0:half, half:] = jnp.zeros((half, half), f32)


def pieces(point):
    low = (point & 255).astype(f32)
    mid = ((point >> 8) & 255).astype(f32)
    top = (point >> 16).astype(f32)
    return low, mid, top


def left_features(point):
    low, mid, top = pieces(point)
    norm = lax.broadcasted_iota(jnp.int32, point.shape, 0) == 3
    one = jnp.ones_like(low)
    zero = jnp.zeros_like(low)
    return jnp.concatenate(
        [low, jnp.where(norm, one, low), mid, jnp.where(norm, one, mid), top, jnp.where(norm, one, zero), zero, zero], 0
    ).astype(bf16)


def right_features(point):
    low, mid, top = pieces(point)
    norm = lax.broadcasted_iota(jnp.int32, point.shape, 0) == 3
    one = jnp.ones_like(low)
    zero = jnp.zeros_like(low)
    return jnp.concatenate(
        [
            jnp.where(norm, one, -2.0 * low),
            jnp.where(norm, low, -512.0 * mid),
            jnp.where(norm, 256.0 * one, -512.0 * low),
            jnp.where(norm, 256.0 * mid, -131072.0 * mid),
            jnp.where(norm, 65536.0 * one, zero),
            jnp.where(norm, 65536.0 * top, zero),
            zero,
            zero,
        ],
        0,
    ).astype(bf16)


def wendland(dist_sq, radius):
    unit = 1.0 / (grid_step * radius)
    dist = dist_sq * lax.rsqrt(jnp.maximum(dist_sq, 1.0))
    rest = jnp.maximum(1.0 - unit * dist, 0.0)
    rest_sq = rest * rest
    return (rest_sq * rest_sq) * (rest_sq * (((35.0 / 3.0 * unit * unit) * dist + 6.0 * unit) * dist + 1.0))


def member(panel_at, block, pattern):
    first = panel_at * SNODE_BLOCKS
    own = (block >= first) & (block < first + SNODE_BLOCKS)
    return jnp.where(own, 1, jnp.where(block < first, 0, pattern[panel_at, block]))


def weight(row, col, pattern):
    value = (row == col).astype(jnp.int32)
    for panel_at in range(PANELS):
        value = value + member(panel_at, row, pattern) * member(panel_at, col, pattern)
    return value.astype(f32)


GROUP = 8


def sums_kernel(radius, per, block_map, pattern, points, out, left, lists, weights):
    nblocks = points.shape[0]
    me = lax.axis_index("prow") * lax.axis_size("pcol") + lax.axis_index("pcol")
    own = [block_map[me * per + b] for b in range(per)]
    right = [right_features(points[me * per + b]) for b in range(per)]

    def scan_block(m, counts):
        left[m] = left_features(points[m])
        after = []
        for b in range(per):
            value = weight(own[b], block_map[m], pattern)
            lists[b, counts[b]] = m
            weights[b, counts[b]] = value
            after.append(counts[b] + (value > 0).astype(jnp.int32))
        return tuple(after)

    counts = lax.fori_loop(0, nblocks, scan_block, (0,) * per)
    for b in range(per):
        for g in range(GROUP):
            lists[b, counts[b] + g] = 0
            weights[b, counts[b] + g] = 0.0

    for b in range(per):

        def group(step, total):
            parts = []
            for g in range(GROUP):
                at = step * GROUP + g
                value = wendland(mm(left[lists[b, at]], right[b], TN), radius)
                parts.append(jnp.sum(value.reshape(BLOCK // 8, 8, BLOCK), axis=0) * weights[b, at])
            return total + functools.reduce(lambda x, y: x + y, parts)

        total = lax.fori_loop(0, (counts[b] + GROUP - 1) // GROUP, group, jnp.zeros((8, BLOCK), f32))
        row = jnp.sum(total, axis=0, keepdims=True)
        for d in range(out.shape[0]):
            out[d, b : b + 1, :] = row


def panels_kernel(
    radius, rows_n, cols_n, block_map, pattern, points, totals, out,
    inverse, panel, left, right_lead, right_cols, scale_rows, scale_lead, scale_cols,
    x_high, x_low, s_high, s_low, x_full, cols_high, cols_low, stage, sems, *work,
):
    nblocks = points.shape[0]
    row_count = nblocks // rows_n
    col_count = nblocks // cols_n
    prow_at = lax.axis_index("prow")
    pcol_at = lax.axis_index("pcol")
    col_base = row_count
    next_base = row_count + col_count
    lead_base = next_base + SNODE_BLOCKS
    slots = lead_base + SNODE_BLOCKS

    def block_of(slot):
        lead = jnp.where(slot < lead_base, slot - next_base + SNODE_BLOCKS, slot - lead_base)
        col = (slot - col_base) * cols_n + pcol_at
        return jnp.where(slot < col_base, slot * rows_n + prow_at, jnp.where(slot < next_base, col, lead))

    def invert(m, carry):
        inverse[block_map[m]] = m
        return carry

    lax.fori_loop(0, nblocks, invert, 0)

    def prepare(slot, carry):
        m = inverse[block_of(slot)]
        left[slot] = left_features(points[m])
        scale = scale_gain * lax.rsqrt(1.0 + totals[pl.ds(m, 1), :])
        scale_rows[slot] = jnp.broadcast_to(scale, (BLOCK, BLOCK)).T
        return carry

    lax.fori_loop(0, slots, prepare, 0)
    for j in range(LEAD):
        m = inverse[j]
        right_lead[:, j * BLOCK : (j + 1) * BLOCK] = right_features(points[m])
        scale_lead[j : j + 1, :] = scale_gain * lax.rsqrt(1.0 + totals[pl.ds(m, 1), :])
    for k in range(col_count):
        m = inverse[k * cols_n + pcol_at]
        right_cols[:, k * BLOCK : (k + 1) * BLOCK] = right_features(points[m])
        scale_cols[k : k + 1, :] = scale_gain * lax.rsqrt(1.0 + totals[pl.ds(m, 1), :])

    def couple(slot, carry):
        g = block_of(slot)
        value = wendland(mm(left[slot], right_lead[...], TN), radius)
        at = pl.ds(pl.multiple_of(slot * BLOCK, BLOCK), BLOCK)
        for j in range(LEAD):
            lanes = slice(j * BLOCK, (j + 1) * BLOCK)
            factor = scale_lead[j : j + 1, :] * weight(g, j, pattern)
            panel[at, lanes] = value[:, lanes] * scale_rows[slot] * factor

        @pl.when(g < LEAD)
        def _():
            lanes = pl.ds(pl.multiple_of(g * BLOCK, BLOCK), BLOCK)
            panel[at, lanes] = panel[at, lanes] + eye(BLOCK)

        return carry

    lax.fori_loop(0, slots, couple, 0)

    chunk = 4 * BLOCK
    factor_diagonal(panel.at[pl.ds(lead_base * BLOCK, WIDTH), pl.ds(0, WIDTH)], x_full, work)
    x_high[...], x_low[...] = split(x_full[...])

    def rows_of(c):
        return pl.ds(pl.multiple_of(c * chunk, chunk), chunk)

    def dot3_with(a, high, low):
        a_high, a_low = split(a)
        return mm(a_high, high, NT) + (mm(a_high, low, NT) + mm(a_low, high, NT))

    def solve_first(c, carry):
        panel[rows_of(c), 0:WIDTH] = dot3_with(panel[rows_of(c), 0:WIDTH], x_high[...], x_low[...])
        return carry

    lax.fori_loop(0, lead_base * BLOCK // chunk, solve_first, 0)
    next_rows = pl.ds(next_base * BLOCK, WIDTH)
    s_high[...], s_low[...] = split(panel[next_rows, 0:WIDTH])
    panel[next_rows, WIDTH:] = panel[next_rows, WIDTH:] - dot3_with(panel[next_rows, 0:WIDTH], s_high[...], s_low[...])
    factor_diagonal(panel.at[next_rows, pl.ds(WIDTH, WIDTH)], x_full, work)
    x_high[...], x_low[...] = split(x_full[...])

    def solve_second(c, carry):
        rest = panel[rows_of(c), WIDTH:] - dot3_with(panel[rows_of(c), 0:WIDTH], s_high[...], s_low[...])
        panel[rows_of(c), WIDTH:] = dot3_with(rest, x_high[...], x_low[...])
        return carry

    lax.fori_loop(0, next_base * BLOCK // chunk, solve_second, 0)
    for i in range(row_count):
        if i * rows_n < SNODE_BLOCKS:

            @pl.when(i * rows_n + prow_at < SNODE_BLOCKS)
            def _(i=i):
                panel[i * BLOCK : (i + 1) * BLOCK, WIDTH:] = jnp.zeros((BLOCK, WIDTH), f32)

    def split_cols(k, carry):
        src = pl.ds(pl.multiple_of((col_base + k) * BLOCK, BLOCK), BLOCK)
        dst = pl.ds(pl.multiple_of(k * BLOCK, BLOCK), BLOCK)
        cols_high[dst, :], cols_low[dst, :] = split(panel[src, :])
        return carry

    lax.fori_loop(0, col_count, split_cols, 0)

    per_slot = BLOCK * col_count
    pair = 2

    def copy_out(step, half):
        at = pl.multiple_of(step * (pair * per_slot), pair * per_slot)
        return pltpu.make_async_copy(stage.at[half], out.at[pl.ds(at, pair * per_slot), :], sems.at[half])

    def trail(step, carry):
        half = step % 2

        @pl.when(step >= 2)
        def _():
            copy_out(step - 2, half).wait()

        at = pl.ds(pl.multiple_of(step * pair * BLOCK, BLOCK), pair * BLOCK)
        update = dot3_with(panel[at, :], cols_high[...], cols_low[...])
        for q in range(pair):
            slot = step * pair + q
            g = block_of(slot)
            keep = (g >= LEAD).astype(f32)
            rows = pl.ds(pl.multiple_of(slot * BLOCK, BLOCK), BLOCK)
            value = wendland(mm(left[slot], right_cols[...], TN), radius)
            for k in range(col_count):
                j = k * cols_n + pcol_at
                lanes = slice(k * BLOCK, (k + 1) * BLOCK)
                factor = scale_cols[k : k + 1, :] * weight(g, j, pattern)
                tile = value[:, lanes] * scale_rows[slot] * factor
                tile = (tile - update[q * BLOCK : (q + 1) * BLOCK, lanes]) * keep
                spots = pl.ds(q * per_slot + k, BLOCK, stride=col_count)
                stage[half, spots, :] = tile
                if k * cols_n < LEAD:

                    @pl.when(j < LEAD)
                    def _(j=j, spots=spots):
                        where = pl.ds(pl.multiple_of(j * BLOCK, BLOCK), BLOCK)
                        stage[half, spots, :] = panel[rows, where]

                @pl.when((j == g) & (j >= LEAD))
                def _(spots=spots):
                    stage[half, spots, :] = stage[half, spots, :] + eye(BLOCK)

        copy_out(step, half).start()
        return carry

    steps = row_count // pair
    lax.fori_loop(0, steps, trail, 0)
    for step in range(max(steps - 2, 0), steps):
        copy_out(step, step % 2).wait()


def local(coords, block_map, pattern):
    rows_n = lax.axis_size("prow")
    cols_n = lax.axis_size("pcol")
    devices = rows_n * cols_n
    nblocks = block_map.shape[0]
    per = nblocks // devices
    row_count = nblocks // rows_n
    col_count = nblocks // cols_n
    radius = (spread_factor / (nblocks * BLOCK)) ** (1.0 / 3.0)
    slots = row_count + col_count + LEAD
    axes = ("prow", "pcol")
    mine = jnp.concatenate([coords, jnp.sum(coords * coords, axis=0, keepdims=True)], 0)
    mine = mine.reshape(4, per, BLOCK).transpose(1, 0, 2)
    points = lax.all_to_all(jnp.broadcast_to(mine[None], (devices, per, 4, BLOCK)), axes, 0, 0, tiled=True)
    points = points.reshape(nblocks, 4, BLOCK)
    smem = pl.BlockSpec(memory_space=pltpu.SMEM)
    vmem = pl.BlockSpec(memory_space=pltpu.VMEM)
    params = pltpu.CompilerParams(vmem_limit_bytes=VMEM_BYTES)
    sums = pl.pallas_call(
        functools.partial(sums_kernel, radius, per),
        out_shape=jax.ShapeDtypeStruct((devices, per, BLOCK), f32),
        in_specs=[smem, smem, vmem],
        out_specs=vmem,
        scratch_shapes=[
            pltpu.VMEM((nblocks, FEATURES, BLOCK), bf16),
            pltpu.SMEM((per, nblocks + GROUP), jnp.int32),
            pltpu.SMEM((per, nblocks + GROUP), f32),
        ],
        compiler_params=params,
        name="sums",
    )(block_map, pattern, points)
    totals = lax.all_to_all(sums, axes, 0, 0, tiled=True).reshape(nblocks, BLOCK)
    out = pl.pallas_call(
        functools.partial(panels_kernel, radius, rows_n, cols_n),
        out_shape=jax.ShapeDtypeStruct((row_count * BLOCK * col_count, BLOCK), f32),
        in_specs=[smem, smem, vmem, vmem],
        out_specs=pl.BlockSpec(memory_space=pl.ANY),
        scratch_shapes=[
            pltpu.SMEM((nblocks,), jnp.int32),
            pltpu.VMEM((slots * BLOCK, PANELS * WIDTH), f32),
            pltpu.VMEM((slots, FEATURES, BLOCK), bf16),
            pltpu.VMEM((FEATURES, LEAD * BLOCK), bf16),
            pltpu.VMEM((FEATURES, col_count * BLOCK), bf16),
            pltpu.VMEM((slots, BLOCK, BLOCK), f32),
            pltpu.VMEM((LEAD, BLOCK), f32),
            pltpu.VMEM((col_count, BLOCK), f32),
            pltpu.VMEM((WIDTH, WIDTH), bf16),
            pltpu.VMEM((WIDTH, WIDTH), bf16),
            pltpu.VMEM((WIDTH, WIDTH), bf16),
            pltpu.VMEM((WIDTH, WIDTH), bf16),
            pltpu.VMEM((WIDTH, WIDTH), f32),
            pltpu.VMEM((col_count * BLOCK, PANELS * WIDTH), bf16),
            pltpu.VMEM((col_count * BLOCK, PANELS * WIDTH), bf16),
            pltpu.VMEM((2, 2 * BLOCK * col_count, BLOCK), f32),
            pltpu.SemaphoreType.DMA((2,)),
        ]
        + [pltpu.VMEM((BLOCK, 2 * BLOCK), f32)] * 4,
        compiler_params=params,
        name="panels",
    )(block_map, pattern, points, totals)
    return out.reshape(row_count, 1, BLOCK, col_count, 1, BLOCK)


def solution(mesh):
    placed = (P(None, ("prow", "pcol")), P(), P())
    return jax.shard_map(
        local,
        mesh=mesh,
        in_specs=placed,
        out_specs=P(None, "prow", None, None, "pcol", None),
        check_vma=False,
    )
```

time: 950 us -> 126 us (0.13)
  waiting for transfers between devices: 306 us -> 0 us
  other arithmetic: 294 us -> 0.71 us
  local copies, waits for them, and re-layouts: 136 us -> 0.73 us
  Pallas kernels: 0 us -> 98.7 us
  matrix products: 89.9 us -> 0 us
  blocking collectives: 94.1 us -> 25.6 us
  between operations: 19.6 us -> 0.19 us
    all_gather x4 -> x0, waiting for transfers between devices: 266 us -> none  [the longest x2 247 us: local(): spread = lax.all_gather(column_piece, 'pcol', axis=2, tiled=True)]
    another operation x37 -> x0, other arithmetic: 247 us -> none  [the longest x30 159 us: local(): lower = jnp.linalg.cholesky(diagonal)]
    pallas_call x0 -> x2, Pallas kernels: none -> 98.7 us  [the longest x1 90.2 us: local(): pl.pallas_call(functools.partial(panels_kernel, radius, rows_n, cols_n),...]
    all_gather x1 -> x0, blocking collectives: 70.7 us -> none  [local(): all_points = lax.all_gather(coords, ('prow', 'pcol'), axis=1, tiled=True)]
    dot_general x2 -> x0, matrix products: 45.7 us -> none  [local(): jnp.einsum('aik,cjk->aicj', trail_rows, col_trail, precision=lax.Precisio...]
    another operation x26 -> x0, matrix products: 44.2 us -> none  [the longest x14 40.5 us: local(): lax.linalg.triangular_solve(lower, flat, left_side=False, lower=True, tra...]
    reshape x5 -> x0, local copies, waits for them, and re-layouts: 41.8 us -> none  [the longest x4 21.3 us: local(): solved.reshape(row_count, BLOCK, width)]
    psum x2 -> x0, waiting for transfers between devices: 40.3 us -> none  [spread_2(): return lax.psum(kept, axis)]
  transfers between devices with their start and end apart: 6 -> 0, of which waited for: 6 -> 0; matrix products, arithmetic and copies ran while one was open for 8% -> 0% of each run, Pallas kernels for 0% -> 0%
where the time goes in v1:
time: 126 us
  Pallas kernels  98.7 us (78%)
  blocking collectives  25.6 us (20%)
    pallas_call x1, Pallas kernels, local(): pl.pallas_call(functools.partial(panels_kernel, radius, rows_n, cols_n),...  90.2 us
    all_to_all x1, blocking collectives, local(): lax.all_to_all(jnp.broadcast_to(mine[None], (devices, per, 4, BLOCK)), ax...  15 us
    all_to_all x1, blocking collectives, local(): lax.all_to_all(sums, axes, 0, 0, tiled=True).reshape(nblocks, BLOCK)  10.6 us
    pallas_call x1, Pallas kernels, local(): pl.pallas_call(functools.partial(sums_kernel, radius, per), out_shape=jax...  8.44 us

profile of v1, /device:TPU:0, one launch (start us, length us, event | category | flops | bytes accessed | tf_op | source)
XLA Modules:
  0.0 125.9 jit_solution(8867261486646364904)
XLA Ops:
  0.0 0.7 multiply_reduce_fusion
  0.7 0.7 concatenate.8
  1.4 15.0 %all_to_all.10 = s32[32,2,4,128]{3,2,1,0:T(4,128)} all-to-all(s32[32,2,4,128]{3,2,1,0:T(4,128)S(1)} %broadcast_in_dim.2), channel_id=1, replica_groups=mesh['prow'=4,'pcol'=8] {'prow','pcol'}, dimensions={0} | all-to-all | bytes 262144 | tf_op jit(solution)/shard_map/all_to_all | solution.py:410
  16.5 8.4 %sums.1 = f32[32,2,128]{2,1,0:T(2,128)} custom-call(s32[64]{0:T(128)} %block_map.3, s32[2,64]{1,0:T(2,128)} %pattern.3, s32[64,4,128]{2,1,0:T(4,128)} %bitcast.8), custom_call_target="tpu_custom_call" | custom-call | tf_op jit(solution)/shard_map/sums/pallas_call | solution.py:415
  24.9 10.6 %all_to_all.11 = f32[32,2,128]{2,1,0:T(2,128)} all-to-all(f32[32,2,128]{2,1,0:T(2,128)} %sums.1), channel_id=1, replica_groups=mesh['prow'=4,'pcol'=8] {'prow','pcol'}, dimensions={0} | all-to-all | bytes 65536 | tf_op jit(solution)/shard_map/all_to_all | solution.py:428
  35.5 90.2 %panels.1 = f32[16384,128]{1,0:T(8,128)} custom-call(s32[64]{0:T(128)} %block_map.3, s32[2,64]{1,0:T(2,128)} %pattern.3, s32[64,4,128]{2,1,0:T(4,128)} %bitcast.9, f32[64,128]{1,0:T(8,128)} %bitcast.10), custom_call_target="tpu_custom_call" | custom-call | tf_op jit(solution)/shard_map/panels/pallas_call | solution.py:429
  (3 shorter events, 0.0 us)
